TPU v7x, 32 devices: a whole 2x2x4 slice. The times are simulated.
32 devices in a mesh: gx: 4 (over y, core), gy: 8 (over z, x).
Axes of the slice: x: 2, y: 2, z: 4, core: 2. Of those that a mesh axis runs over, the one named last changes fastest.
Arguments:
- tokens: bfloat16 [4, 256, 6144], P('gx', None, 'gy'), may hold values from -6 to 6
- norm_gain: float32 [6144], replicated, may hold values from 0.1 to 1.9
- qkv_weight: bfloat16 [6144, 3, 4096], P('gx', None, 'gy'), may hold values from -0.078125 to 0.078125
- up_weight: bfloat16 [6144, 24576], P('gx', 'gy'), may hold values from -0.078125 to 0.078125
- query_gain: float32 [128], replicated, may hold values from 0.1 to 1.9
- key_gain: float32 [128], replicated, may hold values from 0.1 to 1.9
- out_weight: bfloat16 [4096, 6144], P('gy', 'gx'), may hold values from -0.09375 to 0.09375
- down_weight: bfloat16 [24576, 6144], P('gy', 'gx'), may hold values from -0.0390625 to 0.0390625
- attention_keep: int32 [4, 256, 6144], P('gx', None, 'gy'), may hold values 0 or 1
- feedforward_keep: int32 [4, 256, 6144], P('gx', None, 'gy'), may hold values 0 or 1
Outputs:
- block_out: bfloat16 [4, 256, 6144], P('gx', None, 'gy')
All inputs are finite; a program needn't handle non-finite values. No bound on the sum of `attention_keep` or of `feedforward_keep` on one device may be relied on, other than what follows from the above.
Results may differ from a plain program's by a relative error of at most 0.017.
Values may be sent and summed in bfloat16 or wider, within the bound.
A program may use at most 128 MiB of HBM per device.

v0:
```python
import jax
import jax.numpy as jnp
from jax import lax
from jax.sharding import PartitionSpec as P

epsilon = 1e-06
keep_scale = 1.0 / 0.9


def layer_norm(values, gain):
    center = values - jnp.mean(values, axis=-1, keepdims=True)
    variance = jnp.mean(center * center, axis=-1, keepdims=True)
    return center * lax.rsqrt(variance + epsilon) * gain


def head_norm(values, gain):
    row_count = values.shape[0]
    shaped = values.reshape(row_count, -1, gain.shape[0])
    return layer_norm(shaped, gain).reshape(row_count, -1)


def per_device(
    tokens,
    norm_gain,
    qkv_weight,
    up_weight,
    query_gain,
    key_gain,
    out_weight,
    down_weight,
    attention_keep,
    feedforward_keep,
):
    images, seq_len, slice_width = tokens.shape
    whole_rows = lax.all_gather(tokens, "gy", axis=2, tiled=True)
    model_width = whole_rows.shape[2]
    own_rows = images * seq_len
    normed = (
        layer_norm(whole_rows.astype(jnp.float32), norm_gain)
        .astype(jnp.bfloat16)
        .reshape(own_rows, model_width)
    )
    blocks = lax.all_to_all(normed, "gx", split_axis=1, concat_axis=0, tiled=True)
    block_width = blocks.shape[1]
    head_cols = qkv_weight.shape[2]
    head_size = query_gain.shape[0]
    qkv_flat = qkv_weight.reshape(block_width, 3 * head_cols)
    joined = jnp.concatenate([qkv_flat, up_weight], axis=1)
    united = lax.psum_scatter(
        jnp.dot(blocks, joined, preferred_element_type=jnp.float32).astype(jnp.bfloat16),
        "gx",
        scatter_dimension=0,
        tiled=True,
    ).astype(jnp.float32)
    queries = head_norm(united[:, :head_cols], query_gain).astype(jnp.bfloat16)
    keys = head_norm(united[:, head_cols : 2 * head_cols], key_gain).astype(jnp.bfloat16)
    values = united[:, 2 * head_cols : 3 * head_cols].astype(jnp.bfloat16)
    hidden = jax.nn.gelu(united[:, 3 * head_cols :], approximate=False).astype(jnp.bfloat16)
    query_grid = queries.reshape(images, seq_len, -1, head_size)
    key_grid = keys.reshape(images, seq_len, -1, head_size)
    value_grid = values.reshape(images, seq_len, -1, head_size)
    scores = jnp.einsum(
        "bshd,bthd->bhst", query_grid, key_grid, preferred_element_type=jnp.float32
    ) * head_size ** (-0.5)
    raised = jnp.exp(scores)
    weights = (raised / jnp.sum(raised, axis=-1, keepdims=True)).astype(jnp.bfloat16)
    attended = jnp.einsum(
        "bhst,bthd->bshd", weights, value_grid, preferred_element_type=jnp.float32
    )
    attended = attended.astype(jnp.bfloat16).reshape(own_rows, head_cols)
    attention_part = jnp.dot(
        lax.all_gather(attended, "gx", axis=0, tiled=True),
        out_weight,
        preferred_element_type=jnp.float32,
    )
    feedforward_part = jnp.dot(
        lax.all_gather(hidden, "gx", axis=0, tiled=True),
        down_weight,
        preferred_element_type=jnp.float32,
    )
    delivered = (
        lax.all_to_all(
            attention_part.astype(jnp.bfloat16), "gx", split_axis=0, concat_axis=1, tiled=True
        ),
        lax.all_to_all(
            feedforward_part.astype(jnp.bfloat16), "gx", split_axis=0, concat_axis=1, tiled=True
        ),
    )
    rounded = jnp.stack([delivered[0], delivered[1]])
    rounded = lax.optimization_barrier(rounded)
    totals = lax.psum_scatter(
        rounded.astype(jnp.float32).astype(jnp.bfloat16), "gy", scatter_dimension=2, tiled=True
    ).astype(jnp.float32)
    attention_out = totals[0].reshape(images, seq_len, slice_width)
    feedforward_out = totals[1].reshape(images, seq_len, slice_width)
    branches = (
        attention_keep.astype(jnp.float32) * attention_out
        + feedforward_keep.astype(jnp.float32) * feedforward_out
    )
    return (tokens.astype(jnp.float32) + branches * keep_scale).astype(jnp.bfloat16)


def solution(mesh):
    in_specs = (
        P("gx", None, "gy"),
        P(),
        P("gx", None, "gy"),
        P("gx", "gy"),
        P(),
        P(),
        P("gy", "gx"),
        P("gy", "gx"),
        P("gx", None, "gy"),
        P("gx", None, "gy"),
    )
    out_specs = P("gx", None, "gy")
    return jax.shard_map(
        per_device, mesh=mesh, in_specs=in_specs, out_specs=out_specs, check_vma=False
    )
```

profile of v0, /device:TPU:0, one launch (start us, length us, event | category | flops | bytes accessed | tf_op | source)
XLA Modules:
  0.0 534.5 jit_solution(1531559722905003716)
XLA Ops:
  8.6 63.7 %all-gather.4.cloned.1.call-done = bf16[1,256,6144]{1,2,0:T(8,128)(2,1)} async-done(((bf16[1,256,768]{1,2,0:T(8,128)(2,1)}), bf16[1,256,6144]{1,2,0:T(8,128)(2,1)}) %all-gather.4.cloned.1.call-update) | async-done | bytes 3145744 | tf_op jit(solution)/shard_map/all_gather | solution.py:35
  72.3 2.9 convert_reduce_fusion
  76.1 2.3 fusion.11
  78.3 4.7 all-to-all-start
  83.1 6.6 %copy.28 = bf16[1536,3,512]{0,2,1:T(8,128)(2,1)} copy(bf16[1536,3,512]{2,0,1:T(8,128)(2,1)} %param.12) | data formatting | bytes 9437184 | tf_op args[2]
  89.7 6.6 %copy.29 = bf16[1536,1536]{1,0:T(8,128)(2,1)} copy(bf16[1536,1536]{0,1:T(8,128)(2,1)} %bitcast.67) | data formatting | bytes 9437184 | tf_op jit(solution)/shard_map/reshape | solution.py:47
  96.3 23.7 %all-to-all-done = bf16[256,4,1536]{0,2,1:T(8,128)(2,1)} async-done(((bf16[256,4,1536]{0,2,1:T(8,128)(2,1)}), bf16[256,4,1536]{0,2,1:T(8,128)(2,1)}, u32[]{:S(2)}, u32[]{:S(2)}) %all-to-all-start) | async-done | bytes 3145760 | tf_op jit(solution)/shard_map/all_to_all | solution.py:43
  120.0 4.7 copy.27
  124.6 22.6 %fusion.4 = bf16[1024,4608]{1,0:T(8,128)(2,1)} fusion(bf16[1024,1536]{1,0:T(8,128)(2,1)} %bitcast.71, bf16[1536,3072]{1,0:T(8,128)(2,1)} %param.13, bf16[1536,1536]{1,0:T(8,128)(2,1)} %copy.29), kind=kOutput, calls=%fused_computation.4 | convolution fusion | flops 14528544768 | bytes 26738688 | tf_op jit(solution)/shard_map/dot_general | solution.py:50
  148.0 75.2 %reduce-scatter.3.cloned.1.call-done = bf16[256,4608]{1,0:T(8,128)(2,1)} async-done(((bf16[1024,4608]{1,0:T(8,128)(2,1)}), bf16[256,4608]{1,0:T(8,128)(2,1)}) %reduce-scatter.3.cloned.1.call-update) | async-done | bytes 2359312 | tf_op jit(solution)/shard_map/reduce_scatter | solution.py:49
  232.7 8.6 %fusion.14 = bf16[256,3072]{1,0:T(8,128)(2,1)} fusion(f32[256,4608]{1,0:T(8,128)} %copy-done.3), kind=kLoop, calls=%fused_computation.18 | loop fusion | flops 51118080 | bytes 4718592 | tf_op jit(solution)/shard_map/convert_element_type | solution.py:58
  241.3 8.3 %all-gather.6.cloned.1.call-done = bf16[1024,512]{0,1:T(8,128)(2,1)} async-done(((bf16[256,512]{0,1:T(8,128)(2,1)}), bf16[1024,512]{0,1:T(8,128)(2,1)}) %all-gather.6.cloned.1.call-update) | async-done | bytes 1048592 | tf_op jit(solution)/shard_map/all_gather | solution.py:72
  249.6 4.7 convolution_convert_fusion.1
  254.3 4.7 all-to-all-start.1
  259.1 72.0 %all-gather.8.cloned.1.call-done = bf16[1024,3072]{1,0:T(8,128)(2,1)} async-done(((bf16[256,3072]{1,0:T(8,128)(2,1)}), bf16[1024,3072]{1,0:T(8,128)(2,1)}) %all-gather.8.cloned.1.call-update) | async-done | bytes 6291472 | tf_op jit(solution)/shard_map/all_gather | solution.py:77
  331.1 15.6 %convolution_convert_fusion = bf16[1024,1536]{1,0:T(8,128)(2,1)} fusion(bf16[1024,3072]{1,0:T(8,128)(2,1)} %all-gather.8.cloned.1.call-done, bf16[3072,1536]{1,0:T(8,128)(2,1)} %param.17), kind=kOutput, calls=%fused_computation.14 | convolution fusion | flops 9665249280 | bytes 18874368 | tf_op jit(solution)/shard_map/dot_general | solution.py:76
  346.6 4.9 all-to-all-start.2
  351.6 6.0 %copy.34 = bf16[256,4,1536]{2,1,0:T(4,128)(2,1)} copy(bf16[256,4,1536]{2,0,1:T(8,128)(2,1)} %bitcast.11) | data formatting | bytes 6291456 | tf_op jit(solution)/shard_map/all_to_all | solution.py:82
  357.6 6.9 %stack.9 = bf16[1,256,6144]{2,1,0:T(8,128)(2,1)} reshape(bf16[256,4,1536]{2,1,0:T(4,128)(2,1)} %copy.34) | data formatting | bytes 6291456 | tf_op jit(solution)/shard_map/stack | solution.py:89
  364.5 24.0 %all-to-all-done.2 = bf16[4,256,1536]{2,1,0:T(8,128)(2,1)} async-done(((bf16[4,256,1536]{2,1,0:T(8,128)(2,1)}), bf16[4,256,1536]{2,1,0:T(8,128)(2,1)}, u32[]{:S(2)}, u32[]{:S(2)}) %all-to-all-start.2) | async-done | bytes 3145760 | tf_op jit(solution)/shard_map/all_to_all | solution.py:85
  388.5 6.0 %copy.35 = bf16[256,4,1536]{2,1,0:T(4,128)(2,1)} copy(bf16[256,4,1536]{2,0,1:T(8,128)(2,1)} %bitcast.13) | data formatting | bytes 6291456 | tf_op jit(solution)/shard_map/all_to_all | solution.py:85
  394.5 6.9 %stack.10 = bf16[1,256,6144]{2,1,0:T(8,128)(2,1)} reshape(bf16[256,4,1536]{2,1,0:T(4,128)(2,1)} %copy.35) | data formatting | bytes 6291456 | tf_op jit(solution)/shard_map/stack | solution.py:89
  401.4 6.1 %pad_maximum_fusion = bf16[2,256,6144]{2,1,0:T(8,128)(2,1)} fusion(bf16[1,256,6144]{2,1,0:T(8,128)(2,1)} %stack.10, bf16[1,256,6144]{2,1,0:T(8,128)(2,1)} %stack.9), kind=kLoop, calls=%fused_computation.12 | loop fusion | flops 3145728 | bytes 12582912 | tf_op jit(solution)/shard_map/stack | solution.py:89
  407.5 118.2 %reduce-scatter.5.cloned.1.call-done = bf16[2,256,768]{2,1,0:T(8,128)(2,1)} async-done(((bf16[2,256,6144]{2,1,0:T(8,128)(2,1)}), bf16[2,256,768]{2,1,0:T(8,128)(2,1)}) %reduce-scatter.5.cloned.1.call-update) | async-done | bytes 786448 | tf_op jit(solution)/shard_map/reduce_scatter | solution.py:91
  (60 shorter events, 15.4 us)
Async XLA Ops:
  6.5 243.1 %copy-start = (bf16[512,1536]{1,0:T(8,128)(2,1)S(1)}, bf16[512,1536]{1,0:T(8,128)(2,1)}, u32[]{:S(2)}) copy-start(bf16[512,1536]{1,0:T(8,128)(2,1)} %param.16) | copy-start | bytes 4718596
  6.5 65.7 %all-gather.4.cloned.1.call-start = ((), (), s32[]{:S(2)}) async-start(), calls=%async_computation.5 | async-start | bytes 3538944 | tf_op jit(solution)/shard_map/all_gather | solution.py:35
  72.3 2.9 copy-start.2
  72.3 3.8 copy-start.7
  78.3 41.7 %all-to-all-start = ((bf16[256,4,1536]{0,2,1:T(8,128)(2,1)}), bf16[256,4,1536]{0,2,1:T(8,128)(2,1)}, u32[]{:S(2)}, u32[]{:S(2)}) async-start(bf16[256,4,1536]{0,2,1:T(8,128)(2,1)} %bitcast.68), calls=%async_computation | async-start | bytes 6291456 | tf_op jit(solution)/shard_map/all_to_all | solution.py:43
  83.0 140.2 %reduce-scatter.3.cloned.1.call-start = ((), (), s32[]{:S(2)}) async-start(), calls=%async_computation.6 | async-start | bytes 11796480 | tf_op jit(solution)/shard_map/reduce_scatter | solution.py:49
  147.3 0.7 copy-start.8
  147.3 0.7 copy-start.9
  147.3 102.3 %all-gather.6.cloned.1.call-start = ((), (), s32[]{:S(2)}) async-start(), calls=%async_computation.7 | async-start | bytes 1310720 | tf_op jit(solution)/shard_map/all_gather | solution.py:72
  224.3 2.5 slice-start
  229.2 2.1 copy-start.3
  232.7 98.4 %all-gather.8.cloned.1.call-start = ((), (), s32[]{:S(2)}) async-start(), calls=%async_computation.8 | async-start | bytes 7864320 | tf_op jit(solution)/shard_map/all_gather | solution.py:77
  254.3 92.3 %all-to-all-start.1 = ((bf16[4,256,1536]{2,1,0:T(8,128)(2,1)}), bf16[4,256,1536]{2,1,0:T(8,128)(2,1)}, u32[]{:S(2)}, u32[]{:S(2)}) async-start(bf16[4,256,1536]{2,1,0:T(8,128)(2,1)} %bitcast.70), calls=%async_computation.2 | async-start | bytes 6291456 | tf_op jit(solution)/shard_map/all_to_all | solution.py:82
  346.6 41.8 %all-to-all-start.2 = ((bf16[4,256,1536]{2,1,0:T(8,128)(2,1)}), bf16[4,256,1536]{2,1,0:T(8,128)(2,1)}, u32[]{:S(2)}, u32[]{:S(2)}) async-start(bf16[4,256,1536]{2,1,0:T(8,128)(2,1)} %bitcast.69), calls=%async_computation.3 | async-start | bytes 6291456 | tf_op jit(solution)/shard_map/all_to_all | solution.py:85
  351.5 174.2 %reduce-scatter.5.cloned.1.call-start = ((), (), s32[]{:S(2)}) async-start(), calls=%async_computation.9 | async-start | bytes 7077888 | tf_op jit(solution)/shard_map/reduce_scatter | solution.py:91
  407.5 119.4 %copy-start.4 = (bf16[1,256,768]{2,1,0:T(8,128)(2,1)S(1)}, bf16[1,256,768]{2,1,0:T(8,128)(2,1)}, u32[]{:S(2)}) copy-start(bf16[1,256,768]{2,1,0:T(8,128)(2,1)} %param.10) | copy-start | bytes 1179652
  407.5 119.5 %copy-start.5 = (s32[1,256,768]{2,1,0:T(8,128)S(1)}, s32[1,256,768]{2,1,0:T(8,128)}, u32[]{:S(2)}) copy-start(s32[1,256,768]{2,1,0:T(8,128)} %param.19) | copy-start | bytes 2359300
  407.5 119.5 %copy-start.6 = (s32[1,256,768]{2,1,0:T(8,128)S(1)}, s32[1,256,768]{2,1,0:T(8,128)}, u32[]{:S(2)}) copy-start(s32[1,256,768]{2,1,0:T(8,128)} %param.18) | copy-start | bytes 2359300
  407.5 120.4 %copy-start.1 = (bf16[512,1536]{1,0:T(8,128)(2,1)S(1)}, bf16[512,1536]{1,0:T(8,128)(2,1)}, u32[]{:S(2)}) copy-start(bf16[512,1536]{1,0:T(8,128)(2,1)} %param.16) | copy-start | bytes 4718596
Sparse Core Ops, SparseCore 0:
  9.5 62.7 all-gather.3
  147.4 75.6 reduce-scatter.2
  232.8 16.8 all-gather.5
  251.0 79.9 all-gather.7
  407.6 118.0 reduce-scatter.4
where the time goes:
time: 536 us; the launch traced here: 534 us
  waiting for transfers between devices  385 us (72%)
  local copies, waits for them, and re-layouts  49.6 us (9%)
  matrix products  44.2 us (8%)
  other arithmetic  27.6 us (5%)
  starting transfers between devices  14.6 us (3%)
  between operations  13.4 us (2%)
    reduce_scatter x1, waiting for transfers between devices, per_device(): lax.psum_scatter(rounded.astype(jnp.float32).astype(jnp.bfloat16), 'gy',...  118 us
    reduce_scatter x1, waiting for transfers between devices, per_device(): lax.psum_scatter(jnp.dot(blocks, joined, preferred_element_type=jnp.float...  75.2 us
    all_gather x1, waiting for transfers between devices, per_device(): lax.all_gather(hidden, 'gx', axis=0, tiled=True)  72 us
    all_gather x1, waiting for transfers between devices, per_device(): whole_rows = lax.all_gather(tokens, 'gy', axis=2, tiled=True)  63.7 us
    all_to_all x1, waiting for transfers between devices, per_device(): lax.all_to_all(feedforward_part.astype(jnp.bfloat16), 'gx', split_axis=0,...  24 us
    all_to_all x1, waiting for transfers between devices, per_device(): lax.all_to_all(normed, 'gx', split_axis=1, concat_axis=0, tiled=True)  23.7 us
    dot_general x1, matrix products, per_device(): jnp.dot(blocks, joined, preferred_element_type=jnp.float32)  22.6 us
    dot_general x1, matrix products, per_device(): jnp.dot(lax.all_gather(hidden, 'gx', axis=0, tiled=True), down_weight, pr...  15.6 us
  transfers between devices with their start and end apart: 8, of which 7 were waited for; matrix products, arithmetic and copies ran while one was open for 10% of the time, Pallas kernels for 0%

commit v1 on v0

--- a/solution.py
+++ b/solution.py
@@ -32,7 +32,10 @@
     feedforward_keep,
 ):
     images, seq_len, slice_width = tokens.shape
-    whole_rows = lax.all_gather(tokens, "gy", axis=2, tiled=True)
+    copies = []
+    for _ in range(lax.axis_size("gy")):
+        copies.append(tokens)
+    whole_rows = jnp.concatenate(lax.all_to_all(jnp.stack(copies), "gy", 0, 0), axis=2)
     model_width = whole_rows.shape[2]
     own_rows = images * seq_len
     normed = (

time: 536 us -> 555 us (1.035)
  waiting for transfers between devices: 385 us -> 393 us
  starting transfers between devices: 14.6 us -> 22 us
    all_to_all x0 -> x1, waiting for transfers between devices: none -> 70.8 us  [per_device(): lax.all_to_all(jnp.stack(copies), 'gy', 0, 0)]
    all_gather x1 -> x0, waiting for transfers between devices: 63.7 us -> none  [per_device(): whole_rows = lax.all_gather(tokens, 'gy', axis=2, tiled=True)]
    all_to_all x0 -> x1, starting transfers between devices: none -> 7.41 us  [per_device(): lax.all_to_all(jnp.stack(copies), 'gy', 0, 0)]
where the time goes in v1:
time: 555 us; the launch traced here: 553 us
  waiting for transfers between devices  393 us (71%)
  local copies, waits for them, and re-layouts  50.8 us (9%)
  matrix products  44.2 us (8%)
  other arithmetic  30.1 us (5%)
  starting transfers between devices  22 us (4%)
  between operations  13.4 us (2%)
    reduce_scatter x1, waiting for transfers between devices, per_device(): lax.psum_scatter(rounded.astype(jnp.float32).astype(jnp.bfloat16), 'gy',...  118 us
    reduce_scatter x1, waiting for transfers between devices, per_device(): lax.psum_scatter(jnp.dot(blocks, joined, preferred_element_type=jnp.float...  75.6 us
    all_gather x1, waiting for transfers between devices, per_device(): lax.all_gather(hidden, 'gx', axis=0, tiled=True)  72.2 us
    all_to_all x1, waiting for transfers between devices, per_device(): lax.all_to_all(jnp.stack(copies), 'gy', 0, 0)  70.8 us
    all_to_all x1, waiting for transfers between devices, per_device(): lax.all_to_all(feedforward_part.astype(jnp.bfloat16), 'gx', split_axis=0,...  24 us
    all_to_all x1, waiting for transfers between devices, per_device(): lax.all_to_all(normed, 'gx', split_axis=1, concat_axis=0, tiled=True)  23.7 us
    dot_general x1, matrix products, per_device(): jnp.dot(blocks, joined, preferred_element_type=jnp.float32)  22.6 us
    dot_general x1, matrix products, per_device(): jnp.dot(lax.all_gather(hidden, 'gx', axis=0, tiled=True), down_weight, pr...  15.5 us
  transfers between devices with their start and end apart: 8, of which 7 were waited for; matrix products, arithmetic and copies ran while one was open for 10% of the time, Pallas kernels for 0%

profile of v1, /device:TPU:0, one launch (start us, length us, event | category | flops | bytes accessed | tf_op | source)
XLA Modules:
  0.0 553.2 jit_solution(6784538111815050950)
XLA Ops:
  9.7 7.4 %all-to-all-start = ((bf16[8,1,256,768]{2,3,1,0:T(8,128)(2,1)}), bf16[8,1,256,768]{2,3,1,0:T(8,128)(2,1)}, u32[]{:S(2)}, u32[]{:S(2)}) async-start(bf16[8,1,256,768]{2,3,1,0:T(8,128)(2,1)} %stack.8), calls=%async_computation | async-start | bytes 6291456 | tf_op jit(solution)/shard_map/all_to_all | solution.py:38
  17.1 70.8 %all-to-all-done = bf16[8,1,256,768]{2,3,1,0:T(8,128)(2,1)} async-done(((bf16[8,1,256,768]{2,3,1,0:T(8,128)(2,1)}), bf16[8,1,256,768]{2,3,1,0:T(8,128)(2,1)}, u32[]{:S(2)}, u32[]{:S(2)}) %all-to-all-start) | async-done | bytes 3145760 | tf_op jit(solution)/shard_map/all_to_all | solution.py:38
  87.9 2.7 fusion.19
  96.5 4.7 all-to-all-start.1
  101.2 6.6 %copy.31 = bf16[1536,3,512]{0,2,1:T(8,128)(2,1)} copy(bf16[1536,3,512]{2,0,1:T(8,128)(2,1)} %param.12) | data formatting | bytes 9437184 | tf_op args[2]
  107.9 6.6 %copy.32 = bf16[1536,1536]{1,0:T(8,128)(2,1)} copy(bf16[1536,1536]{0,1:T(8,128)(2,1)} %bitcast.82) | data formatting | bytes 9437184 | tf_op jit(solution)/shard_map/reshape | solution.py:50
  114.5 23.7 %all-to-all-done.1 = bf16[256,4,1536]{0,2,1:T(8,128)(2,1)} async-done(((bf16[256,4,1536]{0,2,1:T(8,128)(2,1)}), bf16[256,4,1536]{0,2,1:T(8,128)(2,1)}, u32[]{:S(2)}, u32[]{:S(2)}) %all-to-all-start.1) | async-done | bytes 3145760 | tf_op jit(solution)/shard_map/all_to_all | solution.py:46
  138.2 4.7 copy.30
  142.8 22.6 %fusion.4 = bf16[1024,4608]{1,0:T(8,128)(2,1)} fusion(bf16[1024,1536]{1,0:T(8,128)(2,1)} %bitcast.85, bf16[1536,3072]{1,0:T(8,128)(2,1)} %param.13, bf16[1536,1536]{1,0:T(8,128)(2,1)} %copy.32), kind=kOutput, calls=%fused_computation.4 | convolution fusion | flops 14528544768 | bytes 26738688 | tf_op jit(solution)/shard_map/dot_general | solution.py:53
  166.1 75.6 %reduce-scatter.3.cloned.1.call-done = bf16[256,4608]{1,0:T(8,128)(2,1)} async-done(((bf16[1024,4608]{1,0:T(8,128)(2,1)}), bf16[256,4608]{1,0:T(8,128)(2,1)}) %reduce-scatter.3.cloned.1.call-update) | async-done | bytes 2359312 | tf_op jit(solution)/shard_map/reduce_scatter | solution.py:52
  251.3 8.6 %fusion.11 = bf16[256,3072]{1,0:T(8,128)(2,1)} fusion(f32[256,4608]{1,0:T(8,128)} %copy-done.2), kind=kLoop, calls=%fused_computation.15 | loop fusion | flops 51118080 | bytes 4718592 | tf_op jit(solution)/shard_map/convert_element_type | solution.py:61
  259.9 8.3 %all-gather.3.cloned.1.call-done = bf16[1024,512]{0,1:T(8,128)(2,1)} async-done(((bf16[256,512]{0,1:T(8,128)(2,1)}), bf16[1024,512]{0,1:T(8,128)(2,1)}) %all-gather.3.cloned.1.call-update) | async-done | bytes 1048592 | tf_op jit(solution)/shard_map/all_gather | solution.py:75
  268.2 4.7 convolution_convert_fusion.1
  272.9 4.7 all-to-all-start.2
  277.6 72.2 %all-gather.5.cloned.1.call-done = bf16[1024,3072]{1,0:T(8,128)(2,1)} async-done(((bf16[256,3072]{1,0:T(8,128)(2,1)}), bf16[1024,3072]{1,0:T(8,128)(2,1)}) %all-gather.5.cloned.1.call-update) | async-done | bytes 6291472 | tf_op jit(solution)/shard_map/all_gather | solution.py:80
  349.9 15.5 %convolution_convert_fusion = bf16[1024,1536]{1,0:T(8,128)(2,1)} fusion(bf16[1024,3072]{1,0:T(8,128)(2,1)} %all-gather.5.cloned.1.call-done, bf16[3072,1536]{1,0:T(8,128)(2,1)} %param.17), kind=kOutput, calls=%fused_computation.11 | convolution fusion | flops 9665249280 | bytes 18874368 | tf_op jit(solution)/shard_map/dot_general | solution.py:79
  365.4 4.9 all-to-all-start.3
  370.3 6.0 %copy.37 = bf16[256,4,1536]{2,1,0:T(4,128)(2,1)} copy(bf16[256,4,1536]{2,0,1:T(8,128)(2,1)} %bitcast.15) | data formatting | bytes 6291456 | tf_op jit(solution)/shard_map/all_to_all | solution.py:85
  376.3 6.9 %stack.9 = bf16[1,256,6144]{2,1,0:T(8,128)(2,1)} reshape(bf16[256,4,1536]{2,1,0:T(4,128)(2,1)} %copy.37) | data formatting | bytes 6291456 | tf_op jit(solution)/shard_map/stack | solution.py:92
  383.3 24.0 %all-to-all-done.3 = bf16[4,256,1536]{2,1,0:T(8,128)(2,1)} async-done(((bf16[4,256,1536]{2,1,0:T(8,128)(2,1)}), bf16[4,256,1536]{2,1,0:T(8,128)(2,1)}, u32[]{:S(2)}, u32[]{:S(2)}) %all-to-all-start.3) | async-done | bytes 3145760 | tf_op jit(solution)/shard_map/all_to_all | solution.py:88
  407.3 6.0 %copy.38 = bf16[256,4,1536]{2,1,0:T(4,128)(2,1)} copy(bf16[256,4,1536]{2,0,1:T(8,128)(2,1)} %bitcast.17) | data formatting | bytes 6291456 | tf_op jit(solution)/shard_map/all_to_all | solution.py:88
  413.2 6.9 %stack.10 = bf16[1,256,6144]{2,1,0:T(8,128)(2,1)} reshape(bf16[256,4,1536]{2,1,0:T(4,128)(2,1)} %copy.38) | data formatting | bytes 6291456 | tf_op jit(solution)/shard_map/stack | solution.py:92
  420.2 6.1 %pad_maximum_fusion = bf16[2,256,6144]{2,1,0:T(8,128)(2,1)} fusion(bf16[1,256,6144]{2,1,0:T(8,128)(2,1)} %stack.10, bf16[1,256,6144]{2,1,0:T(8,128)(2,1)} %stack.9), kind=kLoop, calls=%fused_computation.5 | loop fusion | flops 3145728 | bytes 12582912 | tf_op jit(solution)/shard_map/stack | solution.py:92
  426.3 118.1 %reduce-scatter.5.cloned.1.call-done = bf16[2,256,768]{2,1,0:T(8,128)(2,1)} async-done(((bf16[2,256,6144]{2,1,0:T(8,128)(2,1)}), bf16[2,256,768]{2,1,0:T(8,128)(2,1)}) %reduce-scatter.5.cloned.1.call-update) | async-done | bytes 786448 | tf_op jit(solution)/shard_map/reduce_scatter | solution.py:94
  (60 shorter events, 21.5 us)
Async XLA Ops:
  6.5 261.7 %copy-start = (bf16[512,1536]{1,0:T(8,128)(2,1)S(1)}, bf16[512,1536]{1,0:T(8,128)(2,1)}, u32[]{:S(2)}) copy-start(bf16[512,1536]{1,0:T(8,128)(2,1)} %param.16) | copy-start | bytes 4718596
  9.7 7.4 %copy-start.6 = (f32[6144]{0:T(1024)S(1)}, f32[6144]{0:T(1024)}, u32[]{:S(2)}) copy-start(f32[6144]{0:T(1024)} %param.11) | copy-start | bytes 73732
  9.7 78.2 %all-to-all-start = ((bf16[8,1,256,768]{2,3,1,0:T(8,128)(2,1)}), bf16[8,1,256,768]{2,3,1,0:T(8,128)(2,1)}, u32[]{:S(2)}, u32[]{:S(2)}) async-start(bf16[8,1,256,768]{2,3,1,0:T(8,128)(2,1)} %stack.8), calls=%async_computation | async-start | bytes 6291456 | tf_op jit(solution)/shard_map/all_to_all | solution.py:38
  96.5 41.6 %all-to-all-start.1 = ((bf16[256,4,1536]{0,2,1:T(8,128)(2,1)}), bf16[256,4,1536]{0,2,1:T(8,128)(2,1)}, u32[]{:S(2)}, u32[]{:S(2)}) async-start(bf16[256,4,1536]{0,2,1:T(8,128)(2,1)} %multiply_convert_fusion), calls=%async_computation.1 | async-start | bytes 6291456 | tf_op jit(solution)/shard_map/all_to_all | solution.py:46
  101.2 140.5 %reduce-scatter.3.cloned.1.call-start = ((), (), s32[]{:S(2)}) async-start(), calls=%async_computation.6 | async-start | bytes 11796480 | tf_op jit(solution)/shard_map/reduce_scatter | solution.py:52
  165.5 0.7 copy-start.7
  165.5 0.7 copy-start.8
  165.5 102.7 %all-gather.3.cloned.1.call-start = ((), (), s32[]{:S(2)}) async-start(), calls=%async_computation.7 | async-start | bytes 1310720 | tf_op jit(solution)/shard_map/all_gather | solution.py:75
  242.9 2.5 slice-start
  247.7 2.1 copy-start.2
  251.2 98.7 %all-gather.5.cloned.1.call-start = ((), (), s32[]{:S(2)}) async-start(), calls=%async_computation.8 | async-start | bytes 7864320 | tf_op jit(solution)/shard_map/all_gather | solution.py:80
  272.9 92.5 %all-to-all-start.2 = ((bf16[4,256,1536]{2,1,0:T(8,128)(2,1)}), bf16[4,256,1536]{2,1,0:T(8,128)(2,1)}, u32[]{:S(2)}, u32[]{:S(2)}) async-start(bf16[4,256,1536]{2,1,0:T(8,128)(2,1)} %bitcast.84), calls=%async_computation.3 | async-start | bytes 6291456 | tf_op jit(solution)/shard_map/all_to_all | solution.py:85
  365.4 41.8 %all-to-all-start.3 = ((bf16[4,256,1536]{2,1,0:T(8,128)(2,1)}), bf16[4,256,1536]{2,1,0:T(8,128)(2,1)}, u32[]{:S(2)}, u32[]{:S(2)}) async-start(bf16[4,256,1536]{2,1,0:T(8,128)(2,1)} %bitcast.83), calls=%async_computation.4 | async-start | bytes 6291456 | tf_op jit(solution)/shard_map/all_to_all | solution.py:88
  370.3 174.1 %reduce-scatter.5.cloned.1.call-start = ((), (), s32[]{:S(2)}) async-start(), calls=%async_computation.9 | async-start | bytes 7077888 | tf_op jit(solution)/shard_map/reduce_scatter | solution.py:94
  426.2 119.4 %copy-start.3 = (bf16[1,256,768]{2,1,0:T(8,128)(2,1)S(1)}, bf16[1,256,768]{2,1,0:T(8,128)(2,1)}, u32[]{:S(2)}) copy-start(bf16[1,256,768]{2,1,0:T(8,128)(2,1)} %param.10) | copy-start | bytes 1179652
  426.2 119.4 %copy-start.4 = (s32[1,256,768]{2,1,0:T(8,128)S(1)}, s32[1,256,768]{2,1,0:T(8,128)}, u32[]{:S(2)}) copy-start(s32[1,256,768]{2,1,0:T(8,128)} %param.19) | copy-start | bytes 2359300
  426.2 119.4 %copy-start.5 = (s32[1,256,768]{2,1,0:T(8,128)S(1)}, s32[1,256,768]{2,1,0:T(8,128)}, u32[]{:S(2)}) copy-start(s32[1,256,768]{2,1,0:T(8,128)} %param.18) | copy-start | bytes 2359300
  426.3 120.4 %copy-start.1 = (bf16[512,1536]{1,0:T(8,128)(2,1)S(1)}, bf16[512,1536]{1,0:T(8,128)(2,1)}, u32[]{:S(2)}) copy-start(bf16[512,1536]{1,0:T(8,128)(2,1)} %param.16) | copy-start | bytes 4718596
Sparse Core Ops, SparseCore 0:
  165.6 76.0 reduce-scatter.2
  251.3 16.8 all-gather.2
  269.8 80.0 all-gather.4
  426.4 117.9 reduce-scatter.4
